TPU v7x, 512 devices: a whole 4x8x8 slice. The times are simulated.
512 devices in a mesh: context: 128 (over z_hi, x, y, core), chan: 4 (over z_lo).
Axes of the slice: x: 4, y: 8, z: 8 (z_hi: 2, z_lo: 4; z = z_hi * 4 + z_lo), core: 2. Of those that a mesh axis runs over, the one named last changes fastest.
Arguments:
- signal: float32 [64, 131072], P('chan', 'context'), may hold values from -6 to 6
- filter_taps: float32 [131072], P('context'), may hold values from -6 to 6
- skip_gain: float32 [64], P('chan'), may hold values from 0.5 to 1.5
- cotangent: float32 [64, 131072], P('chan', 'context'), may hold values from -6 to 6
Outputs:
- output: float32 [64, 131072], P('chan', 'context')
- grad_signal: float32 [64, 131072], P('chan', 'context')
- grad_filter: float32 [131072], P('context')
All inputs are finite; a program needn't handle non-finite values.
Results may differ from a plain program's by a relative error of at most 0.00013.
Values sent between devices are 32-bit elements; how exact they have to be, the bound alone decides.
A program may use at most 64 MiB of HBM per device.

v0:
```python
import functools
import math

import jax
import jax.numpy as jnp
import numpy as np
from jax import lax
from jax.experimental import pallas as pl
from jax.experimental.pallas import tpu as pltpu
from jax.sharding import PartitionSpec as P

MESH = pl.DeviceIdType.MESH
F32, BF16 = jnp.float32, jnp.bfloat16
BLOCKS, CHANS = 128, 4
A, T = 8, 128
LOCAL = A * T
PAD = 2 * BLOCKS
ROWS = 32
SCALE = 1.0 / (PAD * LOCAL * math.sqrt(BLOCKS * LOCAL))


def as_real(left):
    return np.block([[left.real, -left.imag], [left.imag, left.real]])


def halves(table):
    high = np.asarray(table, np.float32).astype(BF16)
    low = (table - high.astype(np.float64)).astype(np.float32).astype(BF16)
    return np.stack([high, low])


def tables():
    turn = lambda x: np.exp(-2j * np.pi * x)
    t = np.arange(T)
    ka = np.arange(A)
    near = turn(np.outer(t, t) / T)
    far = turn(np.outer(np.arange(PAD), np.arange(BLOCKS)) / PAD)
    fold = 1 + 1j * turn(np.arange(PAD) / PAD)
    back = far.conj().T
    fore = as_real(near)
    last = as_real(near.conj()).T
    spread = np.zeros((2, 128, A * ROWS))
    gather = np.zeros((A * ROWS, 128))
    for k in range(A):
        spread[:, k, k * ROWS : (k + 1) * ROWS] = 1
        spread[1, k, k * ROWS + ROWS // 2 : (k + 1) * ROWS] = -1
        gather[k * ROWS + ROWS // 2 : (k + 1) * ROWS, k] = 1
    twist = turn(np.outer(4 * ka + 1, t) / (4 * LOCAL))
    small = np.zeros((4, A, 128))
    roots = turn(np.outer(ka, 4 * ka + 1) / 32)
    for i, part in enumerate((roots.real, roots.imag, roots.real.T, roots.imag.T)):
        small[i, :, :A] = part
    return dict(
        fore=halves(fore),
        last=halves(last),
        wide=halves(as_real(far)),
        wide_f=halves(as_real(far * fold[:, None])),
        narrow=halves(as_real(back)),
        narrow_g=halves(as_real(back * fold.conj()[None, :])),
        spread=spread.astype(BF16),
        gather=gather.astype(BF16),
        twist=np.stack([twist.real, twist.imag]).astype(np.float32),
        small=small.astype(np.float32),
    )


ROOT = [[complex(np.exp(-2j * np.pi * a * (4 * k + 1) / 32)) for k in range(A)] for a in range(A)]


def split(x):
    high = x.astype(BF16)
    return high, (x - high.astype(F32)).astype(BF16)


def dot(x, y, dims):
    return lax.dot_general(x, y, (dims, ((), ())), preferred_element_type=F32)


NN = ((1,), (0,))
NT = ((1,), (1,))


def product(left, right, dims=NN):
    (lh, ll), (rh, rl) = left, right
    return dot(lh, rh, dims) + (dot(lh, rl, dims) + dot(ll, rh, dims))


def local_forward(signal, cotangent, taps, twist, small, fore):
    parts = []
    for k in range(A):
        re = im = None
        for a in range(A):
            x = jnp.concatenate([signal(a), cotangent(a)], axis=0)
            c = ROOT[a][k]
            re = x * c.real if re is None else re + x * c.real
            im = x * c.imag if im is None else im + x * c.imag
        wr, wi = twist[0][k : k + 1], twist[1][k : k + 1]
        parts.append(jnp.concatenate([re * wr - im * wi, re * wi + im * wr], axis=1))
    z = split(jnp.concatenate(parts, axis=0))
    out = product(fore, z, NT)
    re = im = 0.0
    for a in range(A):
        x = taps[a : a + 1]
        re = re + small[2][:, a : a + 1] * x
        im = im + small[3][:, a : a + 1] * x
    wr, wi = twist
    re, im = re * wr - im * wi, re * wi + im * wr
    zf = jnp.concatenate(
        [
            jnp.concatenate([re, im], axis=1),
            jnp.concatenate([im, -re], axis=1),
            jnp.zeros((128 - 2 * A, 2 * T), F32),
        ],
        axis=0,
    )
    outf = product((fore[0][:T], fore[1][:T]), split(zf), NT)
    return [out[:T, :128], out[:T, 128:], out[T:, :128], out[T:, 128:], outf]


def middle(rows, wide, wide_f, narrow, narrow_g, spread, gather):
    x = jnp.concatenate(
        [jnp.concatenate(rows[0:2], axis=1), jnp.concatenate(rows[2:4], axis=1)], axis=0
    )
    v = product(wide, split(x))
    xf = rows[4]
    xf = jnp.concatenate([xf, pltpu.roll(xf, 128 - A, 1)], axis=0)
    g = product(wide_f, split(xf))
    gh, gl = split(g)
    gr = dot(gh[:PAD], spread[0], NN) + dot(gl[:PAD], spread[0], NN)
    gi = dot(gh[PAD:], spread[1], NN) + dot(gl[PAD:], spread[1], NN)
    vr, vi = v[:PAD], v[PAD:]
    p = jnp.concatenate([vr * gr - vi * gi, vr * gi + vi * gr], axis=0)
    w = product(narrow, split(p))
    turned = jnp.concatenate(
        [pltpu.roll(v[:, :128], ROWS // 2, 1), pltpu.roll(v[:, 128:], ROWS // 2, 1)], axis=1
    )
    sr, si = turned[:PAD], turned[PAD:]
    qh, ql = split(jnp.concatenate([vr * sr + vi * si, vi * sr - vr * si], axis=0))
    d = dot(qh, gather, NN) + dot(ql, gather, NN)
    e = product(narrow_g, split(d))
    grad = e[:BLOCKS] + pltpu.roll(e[BLOCKS:], A, 1)
    return [w[:BLOCKS, :128], w[:BLOCKS, 128:], w[BLOCKS:, :128], w[BLOCKS:, 128:], grad]


def local_inverse(rows, twist, small, last):
    re = jnp.concatenate([rows[0].T, rows[1].T], axis=0)
    im = jnp.concatenate([rows[2].T, rows[3].T], axis=0)
    z = product(split(jnp.concatenate([re, im], axis=1)), last)
    outs = [None] * A
    for k in range(A):
        wr, wi = twist[0][k : k + 1], twist[1][k : k + 1]
        zr, zi = z[k * ROWS : (k + 1) * ROWS, :T], z[k * ROWS : (k + 1) * ROWS, T:]
        yr, yi = zr * wr + zi * wi, zi * wr - zr * wi
        for a in range(A):
            c = ROOT[a][k].conjugate()
            term = yr * (c.real * SCALE) - yi * (c.imag * SCALE)
            outs[a] = term if outs[a] is None else outs[a] + term
    g = rows[4].T
    zg = product(split(jnp.concatenate([g[:A], g[A : 2 * A]], axis=1)), last)
    wr, wi = twist
    zr, zi = zg[:, :T], zg[:, T:]
    yr, yi = zr * wr + zi * wi, zi * wr - zr * wi
    grad = 0.0
    for k in range(A):
        grad = grad + (small[0][:, k : k + 1] * yr[k : k + 1] + small[1][:, k : k + 1] * yi[k : k + 1])
    return outs, grad * SCALE


NAMES = ("twist", "small", "fore", "wide", "wide_f", "narrow", "narrow_g", "spread", "gather", "last")
SLOT = 8
USED = 5


def kernel(sig, cot, taps, *refs):
    n = len(NAMES)
    sources, (conv_out, grad_out) = refs[:n], refs[n : n + 2]
    held = dict(zip(NAMES, refs[n + 2 : 2 * n + 2]))
    out1, in1, out2, in2, own, others, load, s1, r1, s2, r2, s3, r3 = refs[2 * n + 2 :]
    me, chan = lax.axis_index("context"), lax.axis_index("chan")

    barrier = pltpu.get_barrier_semaphore()

    def greet(i, c):
        pl.semaphore_signal(
            barrier, inc=1, device_id=(lax.rem(me + i, BLOCKS), chan), device_id_type=MESH
        )
        return c

    lax.fori_loop(1, BLOCKS, greet, 0)
    for i in range(1, CHANS):
        pl.semaphore_signal(
            barrier, inc=1, device_id=(me, lax.rem(chan + i, CHANS)), device_id_type=MESH
        )

    loads = {
        name: pltpu.make_async_copy(source, held[name], load.at[i])
        for i, (name, source) in enumerate(zip(NAMES, sources))
    }
    for copy in loads.values():
        copy.start()

    def table(name):
        loads[name].wait()
        return held[name][...]

    def exchange(source, target, sent, arrived):
        def slot(ref, i):
            return ref.at[pl.ds(pl.multiple_of(i * SLOT, SLOT), USED)]

        def send(i, c):
            peer = lax.rem(me + i, BLOCKS)
            pltpu.make_async_remote_copy(
                src_ref=slot(source, peer),
                dst_ref=slot(target, me),
                send_sem=sent,
                recv_sem=arrived,
                device_id=(peer, chan),
                device_id_type=MESH,
            ).start()
            return c

        lax.fori_loop(1, BLOCKS, send, 0)
        stay = pltpu.make_async_copy(slot(source, me), slot(target, me), sent)
        stay.start()

        whole = source.at[pl.ds(0, BLOCKS * USED)]
        pltpu.make_async_copy(whole, whole, sent).wait()
        part = source.at[pl.ds(0, (BLOCKS - 1) * USED)]
        pltpu.make_async_copy(part, part, arrived).wait()

    def put(ref, rows):
        for i, row in enumerate(rows):
            ref[pl.ds(i, BLOCKS, stride=SLOT), :] = row

    def take(ref):
        return [ref[pl.ds(i, BLOCKS, stride=SLOT), :] for i in range(USED)]

    twist, small = table("twist"), table("small")
    put(
        out1,
        local_forward(
            lambda a: sig[:, a * T : (a + 1) * T],
            lambda a: cot[:, a * T : (a + 1) * T],
            taps[...],
            twist,
            small,
            table("fore"),
        ),
    )
    pl.semaphore_wait(barrier, BLOCKS - 1 + CHANS - 1)
    exchange(out1, in1, s1, r1)
    names = ("wide", "wide_f", "narrow", "narrow_g", "spread", "gather")
    put(out2, middle(take(in1), *[table(name) for name in names]))
    exchange(out2, in2, s2, r2)
    outs, grad = local_inverse(take(in2), held["twist"][...], held["small"][...], table("last"))
    own[...] = grad
    copies = []
    for i in range(1, CHANS):
        copies.append(
            pltpu.make_async_remote_copy(
                src_ref=own,
                dst_ref=others.at[i - 1],
                send_sem=s3.at[i - 1],
                recv_sem=r3.at[i - 1],
                device_id=(me, lax.rem(chan + i, CHANS)),
                device_id_type=MESH,
            )
        )
    for copy in copies:
        copy.start()
    for a in range(A):
        conv_out[:, a * T : (a + 1) * T] = outs[a]
    for copy in copies:
        copy.wait()
    pieces = [own[...]] + [others[i] for i in range(CHANS - 1)]
    total = 0.0
    for g in range(CHANS):
        at = lax.rem(chan - g + CHANS, CHANS)
        piece = pieces[0]
        for i in range(1, CHANS):
            piece = jnp.where(at == i, pieces[i], piece)
        total = total + piece
    grad_out[...] = total


def body(signal, filter_taps, skip_gain, cotangent):
    made = tables()
    consts = [jnp.asarray(made[name]) for name in NAMES]
    whole = pl.BlockSpec(memory_space=pltpu.VMEM)
    conv, grad = pl.pallas_call(
        kernel,
        out_shape=(
            jax.ShapeDtypeStruct((ROWS, LOCAL), F32),
            jax.ShapeDtypeStruct((A, T), F32),
        ),
        in_specs=[whole] * 3 + [pl.BlockSpec(memory_space=pl.ANY)] * len(NAMES),
        out_specs=(whole, whole),
        scratch_shapes=[pltpu.VMEM(c.shape, c.dtype) for c in consts]
        + [pltpu.VMEM((BLOCKS * SLOT, 128), F32)] * 4
        + [pltpu.VMEM((A, T), F32), pltpu.VMEM((CHANS - 1, A, T), F32)]
        + [pltpu.SemaphoreType.DMA((len(NAMES),))]
        + [pltpu.SemaphoreType.DMA] * 4
        + [pltpu.SemaphoreType.DMA((CHANS - 1,))] * 2,
        compiler_params=pltpu.CompilerParams(collective_id=0, has_side_effects=True),
        name="hyena",
    )(signal, cotangent, filter_taps.reshape(A, T), *consts)
    gain = skip_gain[:, None]
    half = ROWS // 2
    return (
        conv[:half] + gain * signal,
        conv[half:] + gain * cotangent,
        grad.reshape(LOCAL),
    )


def solution(mesh):
    return jax.shard_map(
        body,
        mesh=mesh,
        in_specs=(P("chan", "context"), P("context"), P("chan"), P("chan", "context")),
        out_specs=(P("chan", "context"), P("chan", "context"), P("context")),
        check_vma=False,
    )
```

profile of v0, /device:TPU:1, one launch (start us, length us, event | category | flops | bytes accessed | tf_op | source)
XLA Modules:
  0.0 55.0 jit_solution(3403491118964842434)
XLA Ops:
  0.6 0.0 copy-start
  0.6 0.0 copy-start.1
  0.7 51.5 %hyena.1 = (f32[32,1024]{1,0:T(8,128)}, f32[8,128]{1,0:T(8,128)}) custom-call(f32[16,1024]{1,0:T(8,128)} %sig.1, f32[16,1024]{1,0:T(8,128)} %cot.1, f32[8,128]{1,0:T(8,128)} %bitcast.2, f32[2,8,128]{2,1,0:T(8,128)} %constant.18.clone.refs_0_, f32[4,8,128]{2,1,0:T(8,128)} %constant.19.clone.refs_1_, bf16[2,256,256]{2,1,0:T(8,128)(2,1)} %constant.20.clone.refs_2_.refs_9_, ...), custom_call_target="tpu_custom_call" | custom-call | tf_op jit(solution)/shard_map/hyena/pallas_call | solution.py:290
  52.1 0.0 copy-start.3
  52.1 0.0 copy-done
  52.1 0.0 copy-done.1
  52.2 0.6 %copy-done.3 = f32[16]{0:T(128)S(1)} copy-done((f32[16]{0:T(128)S(1)}, f32[16]{0:T(128)}, u32[]{:S(2)}) %copy-start.3) | copy-done | bytes 88
  52.8 0.0 copy-start.2
  52.8 1.6 %multiply_add_fusion = (f32[16,1024]{1,0:T(8,128)}, f32[16,1024]{1,0:T(8,128)}) fusion(f32[16,1024]{1,0:T(8,128)S(1)} %copy-done, f32[32,1024]{1,0:T(8,128)} %get-tuple-element.5, f32[16]{0:T(128)S(1)} %copy-done.3, f32[16,1024]{1,0:T(8,128)S(1)} %copy-done.1), kind=kLoop, calls=%fused_computation | loop fusion | flops 65536 | bytes 393280 | tf_op jit(solution)/shard_map/add | solution.py:311
  54.4 0.0 copy-done.2
  54.4 0.6 %copy.18 = f32[1024]{0:T(1024)} copy(f32[1024]{0:T(1024)S(1)} %bitcast.3) | data formatting | bytes 8192
Async XLA Ops:
  0.6 51.5 %copy-start = (f32[16,1024]{1,0:T(8,128)S(1)}, f32[16,1024]{1,0:T(8,128)}, u32[]{:S(2)}) copy-start(f32[16,1024]{1,0:T(8,128)} %cot.1) | copy-start | bytes 196612
  0.6 51.5 %copy-start.1 = (f32[16,1024]{1,0:T(8,128)S(1)}, f32[16,1024]{1,0:T(8,128)}, u32[]{:S(2)}) copy-start(f32[16,1024]{1,0:T(8,128)} %sig.1) | copy-start | bytes 196612
  52.1 0.7 %copy-start.3 = (f32[16]{0:T(128)S(1)}, f32[16]{0:T(128)}, u32[]{:S(2)}) copy-start(f32[16]{0:T(128)} %param.16) | copy-start | bytes 196
  52.8 1.6 %copy-start.2 = (f32[8,128]{1,0:T(8,128)S(1)}, f32[8,128]{1,0:T(8,128)}, u32[]{:S(2)}) copy-start(f32[8,128]{1,0:T(8,128)} %get-tuple-element.6) | copy-start | bytes 12292
where the time goes:
time: 55.2 us; the launch traced here: 55 us
  Pallas kernels  51.5 us (93%)
  other arithmetic  1.6 us (3%)
  local copies, waits for them, and re-layouts  1.24 us (2%)
  between operations  0.68 us (1%)
    pallas_call x1, Pallas kernels, body(): pl.pallas_call(kernel, out_shape=(jax.ShapeDtypeStruct((ROWS, LOCAL), F32...  51.5 us
    add x1, other arithmetic, body(): conv[half:] + gain * cotangent  1.6 us
    unnamed x9, local copies, waits for them, and re-layouts  1.24 us

commit v1 on v0

--- a/solution.py
+++ b/solution.py
@@ -117,20 +117,26 @@
     return [out[:T, :128], out[:T, 128:], out[T:, :128], out[T:, 128:], outf]
 
 
-def middle(rows, wide, wide_f, narrow, narrow_g, spread, gather):
+def along_blocks(rows, wide):
     x = jnp.concatenate(
         [jnp.concatenate(rows[0:2], axis=1), jnp.concatenate(rows[2:4], axis=1)], axis=0
     )
-    v = product(wide, split(x))
-    xf = rows[4]
+    return product(wide, split(x))
+
+
+def convolve(v, xf, wide_f, narrow, spread):
     xf = jnp.concatenate([xf, pltpu.roll(xf, 128 - A, 1)], axis=0)
-    g = product(wide_f, split(xf))
-    gh, gl = split(g)
+    gh, gl = split(product(wide_f, split(xf)))
     gr = dot(gh[:PAD], spread[0], NN) + dot(gl[:PAD], spread[0], NN)
     gi = dot(gh[PAD:], spread[1], NN) + dot(gl[PAD:], spread[1], NN)
     vr, vi = v[:PAD], v[PAD:]
     p = jnp.concatenate([vr * gr - vi * gi, vr * gi + vi * gr], axis=0)
     w = product(narrow, split(p))
+    return [w[:BLOCKS, :128], w[:BLOCKS, 128:], w[BLOCKS:, :128], w[BLOCKS:, 128:]]
+
+
+def correlate(v, narrow_g, gather):
+    vr, vi = v[:PAD], v[PAD:]
     turned = jnp.concatenate(
         [pltpu.roll(v[:, :128], ROWS // 2, 1), pltpu.roll(v[:, 128:], ROWS // 2, 1)], axis=1
     )
@@ -138,11 +144,10 @@
     qh, ql = split(jnp.concatenate([vr * sr + vi * si, vi * sr - vr * si], axis=0))
     d = dot(qh, gather, NN) + dot(ql, gather, NN)
     e = product(narrow_g, split(d))
-    grad = e[:BLOCKS] + pltpu.roll(e[BLOCKS:], A, 1)
-    return [w[:BLOCKS, :128], w[:BLOCKS, 128:], w[BLOCKS:, :128], w[BLOCKS:, 128:], grad]
-
-
-def local_inverse(rows, twist, small, last):
+    return e[:BLOCKS] + pltpu.roll(e[BLOCKS:], A, 1)
+
+
+def local_inverse(rows, twist, last):
     re = jnp.concatenate([rows[0].T, rows[1].T], axis=0)
     im = jnp.concatenate([rows[2].T, rows[3].T], axis=0)
     z = product(split(jnp.concatenate([re, im], axis=1)), last)
@@ -155,7 +160,11 @@
             c = ROOT[a][k].conjugate()
             term = yr * (c.real * SCALE) - yi * (c.imag * SCALE)
             outs[a] = term if outs[a] is None else outs[a] + term
-    g = rows[4].T
+    return outs
+
+
+def inverse_taps(row, twist, small, last):
+    g = row.T
     zg = product(split(jnp.concatenate([g[:A], g[A : 2 * A]], axis=1)), last)
     wr, wi = twist
     zr, zi = zg[:, :T], zg[:, T:]
@@ -163,19 +172,19 @@
     grad = 0.0
     for k in range(A):
         grad = grad + (small[0][:, k : k + 1] * yr[k : k + 1] + small[1][:, k : k + 1] * yi[k : k + 1])
-    return outs, grad * SCALE
-
-
-NAMES = ("twist", "small", "fore", "wide", "wide_f", "narrow", "narrow_g", "spread", "gather", "last")
+    return grad * SCALE
+
+
+NAMES = ("signal", "cotangent", "taps", "gain", "twist", "small", "fore", "wide", "wide_f", "narrow", "narrow_g", "spread", "gather", "last")
 SLOT = 8
-USED = 5
-
-
-def kernel(sig, cot, taps, *refs):
+LIMIT = 60 * 1024 * 1024
+
+
+def kernel(*refs):
     n = len(NAMES)
-    sources, (conv_out, grad_out) = refs[:n], refs[n : n + 2]
-    held = dict(zip(NAMES, refs[n + 2 : 2 * n + 2]))
-    out1, in1, out2, in2, own, others, load, s1, r1, s2, r2, s3, r3 = refs[2 * n + 2 :]
+    sources, (out_s, out_c, out_f) = refs[:n], refs[n : n + 3]
+    held = dict(zip(NAMES, refs[n + 3 : 2 * n + 3]))
+    out1, in1, out2, in2, own, others, load, s1, r1, sg, rg, s2, r2, s3, r3 = refs[2 * n + 3 :]
     me, chan = lax.axis_index("context"), lax.axis_index("chan")
 
     barrier = pltpu.get_barrier_semaphore()
@@ -203,15 +212,15 @@
         loads[name].wait()
         return held[name][...]
 
-    def exchange(source, target, sent, arrived):
-        def slot(ref, i):
-            return ref.at[pl.ds(pl.multiple_of(i * SLOT, SLOT), USED)]
-
+    def slot(ref, i, first, count):
+        return ref.at[pl.ds(pl.multiple_of(i * SLOT, SLOT) + first, count)]
+
+    def start(source, target, sent, arrived, first, count):
         def send(i, c):
             peer = lax.rem(me + i, BLOCKS)
             pltpu.make_async_remote_copy(
-                src_ref=slot(source, peer),
-                dst_ref=slot(target, me),
+                src_ref=slot(source, peer, first, count),
+                dst_ref=slot(target, me, first, count),
                 send_sem=sent,
                 recv_sem=arrived,
                 device_id=(peer, chan),
@@ -219,41 +228,63 @@
             ).start()
             return c
 
+        pltpu.make_async_copy(
+            slot(source, me, first, count), slot(target, me, first, count), sent
+        ).start()
         lax.fori_loop(1, BLOCKS, send, 0)
-        stay = pltpu.make_async_copy(slot(source, me), slot(target, me), sent)
-        stay.start()
-
-        whole = source.at[pl.ds(0, BLOCKS * USED)]
+
+    def finish(source, sent, arrived, count):
+        whole = source.at[pl.ds(0, BLOCKS * count)]
         pltpu.make_async_copy(whole, whole, sent).wait()
-        part = source.at[pl.ds(0, (BLOCKS - 1) * USED)]
+        part = source.at[pl.ds(0, (BLOCKS - 1) * count)]
         pltpu.make_async_copy(part, part, arrived).wait()
 
     def put(ref, rows):
         for i, row in enumerate(rows):
             ref[pl.ds(i, BLOCKS, stride=SLOT), :] = row
 
-    def take(ref):
-        return [ref[pl.ds(i, BLOCKS, stride=SLOT), :] for i in range(USED)]
-
+    def take(ref, first, last):
+        return [ref[pl.ds(i, BLOCKS, stride=SLOT), :] for i in range(first, last)]
+
+    for name in ("signal", "cotangent"):
+        loads[name].wait()
+    sig, cot = held["signal"], held["cotangent"]
+    taps = table("taps")
+    loads["gain"].wait()
     twist, small = table("twist"), table("small")
     put(
         out1,
         local_forward(
             lambda a: sig[:, a * T : (a + 1) * T],
             lambda a: cot[:, a * T : (a + 1) * T],
-            taps[...],
+            taps,
             twist,
             small,
             table("fore"),
         ),
     )
+    for name in ("wide", "wide_f", "narrow", "narrow_g", "spread", "gather", "last"):
+        loads[name].wait()
     pl.semaphore_wait(barrier, BLOCKS - 1 + CHANS - 1)
-    exchange(out1, in1, s1, r1)
-    names = ("wide", "wide_f", "narrow", "narrow_g", "spread", "gather")
-    put(out2, middle(take(in1), *[table(name) for name in names]))
-    exchange(out2, in2, s2, r2)
-    outs, grad = local_inverse(take(in2), held["twist"][...], held["small"][...], table("last"))
-    own[...] = grad
+    start(out1, in1, s1, r1, 0, 5)
+    finish(out1, s1, r1, 5)
+
+    rows = take(in1, 0, 5)
+    v = along_blocks(rows, held["wide"][...])
+    out2[pl.ds(4, BLOCKS, stride=SLOT), :] = correlate(
+        v, held["narrow_g"][...], held["gather"][...]
+    )
+    start(out2, in2, sg, rg, 4, 1)
+    put(
+        out2,
+        convolve(v, rows[4], held["wide_f"][...], held["narrow"][...], held["spread"][...]),
+    )
+    start(out2, in2, s2, r2, 0, 4)
+
+    finish(out2, sg, rg, 1)
+    own[...] = inverse_taps(
+        take(in2, 4, 5)[0], held["twist"][...], held["small"][...], held["last"][...]
+    )
     copies = []
     for i in range(1, CHANS):
         copies.append(
@@ -268,8 +299,18 @@
         )
     for copy in copies:
         copy.start()
+
+    finish(out2, s2, r2, 4)
+    outs = local_inverse(take(in2, 0, 4), held["twist"][...], held["last"][...])
+    half = ROWS // 2
+    row = lax.broadcasted_iota(jnp.int32, (half, T), 0)
+    column = jnp.zeros((half, T), F32)
+    for r in range(half):
+        column = jnp.where(row == r, held["gain"][r], column)
     for a in range(A):
-        conv_out[:, a * T : (a + 1) * T] = outs[a]
+        at = slice(a * T, (a + 1) * T)
+        out_s[:, at] = outs[a][:half] + column * sig[:, at]
+        out_c[:, at] = outs[a][half:] + column * cot[:, at]
     for copy in copies:
         copy.wait()
     pieces = [own[...]] + [others[i] for i in range(CHANS - 1)]
@@ -280,37 +321,37 @@
         for i in range(1, CHANS):
             piece = jnp.where(at == i, pieces[i], piece)
         total = total + piece
-    grad_out[...] = total
+    out_f[...] = total
 
 
 def body(signal, filter_taps, skip_gain, cotangent):
     made = tables()
-    consts = [jnp.asarray(made[name]) for name in NAMES]
-    whole = pl.BlockSpec(memory_space=pltpu.VMEM)
-    conv, grad = pl.pallas_call(
+    consts = [signal, cotangent, filter_taps.reshape(A, T), skip_gain]
+    consts += [jnp.asarray(made[name]) for name in NAMES[4:]]
+    vmem = pl.BlockSpec(memory_space=pltpu.VMEM)
+    hbm = pl.BlockSpec(memory_space=pltpu.HBM)
+    block = jax.ShapeDtypeStruct((ROWS // 2, LOCAL), F32)
+    line = jax.ShapeDtypeStruct((A, T), F32)
+    output, grad_signal, grad_filter = pl.pallas_call(
         kernel,
-        out_shape=(
-            jax.ShapeDtypeStruct((ROWS, LOCAL), F32),
-            jax.ShapeDtypeStruct((A, T), F32),
-        ),
-        in_specs=[whole] * 3 + [pl.BlockSpec(memory_space=pl.ANY)] * len(NAMES),
-        out_specs=(whole, whole),
-        scratch_shapes=[pltpu.VMEM(c.shape, c.dtype) for c in consts]
+        out_shape=(block, block, line),
+        in_specs=[hbm] * len(NAMES),
+        out_specs=(vmem,) * 3,
+        scratch_shapes=[
+            (pltpu.SMEM if name == "gain" else pltpu.VMEM)(c.shape, c.dtype)
+            for name, c in zip(NAMES, consts)
+        ]
         + [pltpu.VMEM((BLOCKS * SLOT, 128), F32)] * 4
         + [pltpu.VMEM((A, T), F32), pltpu.VMEM((CHANS - 1, A, T), F32)]
         + [pltpu.SemaphoreType.DMA((len(NAMES),))]
-        + [pltpu.SemaphoreType.DMA] * 4
+        + [pltpu.SemaphoreType.DMA] * 6
         + [pltpu.SemaphoreType.DMA((CHANS - 1,))] * 2,
-        compiler_params=pltpu.CompilerParams(collective_id=0, has_side_effects=True),
+        compiler_params=pltpu.CompilerParams(
+            collective_id=0, has_side_effects=True, vmem_limit_bytes=LIMIT
+        ),
         name="hyena",
-    )(signal, cotangent, filter_taps.reshape(A, T), *consts)
-    gain = skip_gain[:, None]
-    half = ROWS // 2
-    return (
-        conv[:half] + gain * signal,
-        conv[half:] + gain * cotangent,
-        grad.reshape(LOCAL),
-    )
+    )(*consts)
+    return output, grad_signal, grad_filter.reshape(LOCAL)
 
 
 def solution(mesh):

time: 55.2 us -> 51.9 us (0.940)
  Pallas kernels: 51.5 us -> 48.3 us
  other arithmetic: 1.6 us -> 0 us
  local copies, waits for them, and re-layouts: 1.24 us -> 2.78 us
    pallas_call x1, Pallas kernels: 51.5 us -> 48.3 us  [body(): pl.pallas_call(kernel, out_shape=(block, block, line), in_specs=[hbm] * l...]
    add x1 -> x0, other arithmetic: 1.6 us -> none  [body(): conv[half:] + gain * cotangent]
    unnamed x9 -> x7, local copies, waits for them, and re-layouts: 1.24 us -> 2.78 us
where the time goes in v1:
time: 51.9 us; the launch traced here: 51.7 us
  Pallas kernels  48.3 us (93%)
  local copies, waits for them, and re-layouts  2.78 us (5%)
  between operations  0.65 us (1%)
    pallas_call x1, Pallas kernels, body(): pl.pallas_call(kernel, out_shape=(block, block, line), in_specs=[hbm] * l...  48.3 us
    unnamed x7, local copies, waits for them, and re-layouts  2.78 us

profile of v1, /device:TPU:1, one launch (start us, length us, event | category | flops | bytes accessed | tf_op | source)
XLA Modules:
  0.0 51.7 jit_solution(9353357454074109125)
XLA Ops:
  0.6 48.3 %hyena.1 = (f32[16,1024]{1,0:T(8,128)}, f32[16,1024]{1,0:T(8,128)}, f32[8,128]{1,0:T(8,128)}) custom-call(f32[16,1024]{1,0:T(8,128)} %refs_0_.1, f32[16,1024]{1,0:T(8,128)} %refs_1_.1, f32[8,128]{1,0:T(8,128)} %bitcast.2, f32[16]{0:T(128)} %refs_3_.1, f32[2,8,128]{2,1,0:T(8,128)} %constant.18.clone.refs_4_, f32[4,8,128]{2,1,0:T(8,128)} %constant.19.clone.refs_5_, ...), custom_call_target="tpu_custom_call" | custom-call | tf_op jit(solution)/shard_map/hyena/pallas_call | solution.py:335
  48.9 0.0 copy-start
  48.9 1.5 %copy.20 = f32[16,1024]{1,0:T(8,128)} copy(f32[16,1024]{1,0:T(8,128)} %get-tuple-element.12) | data formatting | bytes 131072
  50.4 0.0 copy-done
  50.4 0.0 copy-start.1
  50.4 0.6 %copy.21 = f32[16,1024]{1,0:T(8,128)} copy(f32[16,1024]{1,0:T(8,128)S(1)} %copy-done) | data formatting | bytes 131072
  51.1 0.0 copy-done.1
  51.1 0.6 %copy.22 = f32[1024]{0:T(1024)} copy(f32[1024]{0:T(1024)S(1)} %bitcast.3) | data formatting | bytes 8192
Async XLA Ops:
  48.9 1.5 %copy-start = (f32[16,1024]{1,0:T(8,128)S(1)}, f32[16,1024]{1,0:T(8,128)}, u32[]{:S(2)}) copy-start(f32[16,1024]{1,0:T(8,128)} %get-tuple-element.13) | copy-start | bytes 196612
  50.4 0.7 %copy-start.1 = (f32[8,128]{1,0:T(8,128)S(1)}, f32[8,128]{1,0:T(8,128)}, u32[]{:S(2)}) copy-start(f32[8,128]{1,0:T(8,128)} %get-tuple-element.8) | copy-start | bytes 12292

commit v2 on v1

--- a/solution.py
+++ b/solution.py
@@ -127,8 +127,9 @@
 def convolve(v, xf, wide_f, narrow, spread):
     xf = jnp.concatenate([xf, pltpu.roll(xf, 128 - A, 1)], axis=0)
     gh, gl = split(product(wide_f, split(xf)))
-    gr = dot(gh[:PAD], spread[0], NN) + dot(gl[:PAD], spread[0], NN)
-    gi = dot(gh[PAD:], spread[1], NN) + dot(gl[PAD:], spread[1], NN)
+    gb = jnp.concatenate([gh, gl], axis=1)
+    gr = dot(gb[:PAD], jnp.concatenate([spread[0], spread[0]], axis=0), NN)
+    gi = dot(gb[PAD:], jnp.concatenate([spread[1], spread[1]], axis=0), NN)
     vr, vi = v[:PAD], v[PAD:]
     p = jnp.concatenate([vr * gr - vi * gi, vr * gi + vi * gr], axis=0)
     w = product(narrow, split(p))
@@ -177,6 +178,7 @@
 
 NAMES = ("signal", "cotangent", "taps", "gain", "twist", "small", "fore", "wide", "wide_f", "narrow", "narrow_g", "spread", "gather", "last")
 SLOT = 8
+GROUP = 7
 LIMIT = 60 * 1024 * 1024
 
 
@@ -189,13 +191,23 @@
 
     barrier = pltpu.get_barrier_semaphore()
 
-    def greet(i, c):
-        pl.semaphore_signal(
-            barrier, inc=1, device_id=(lax.rem(me + i, BLOCKS), chan), device_id_type=MESH
-        )
-        return c
-
-    lax.fori_loop(1, BLOCKS, greet, 0)
+    def each_peer(visit):
+        def turn(i, c):
+            for j in range(GROUP):
+                peer = me + (i * GROUP + j + 1)
+                visit(jnp.where(peer >= BLOCKS, peer - BLOCKS, peer))
+            return c
+
+        whole = (BLOCKS - 1) // GROUP
+        lax.fori_loop(0, whole, turn, 0)
+        for j in range(whole * GROUP + 1, BLOCKS):
+            peer = me + j
+            visit(jnp.where(peer >= BLOCKS, peer - BLOCKS, peer))
+
+    def greet(peer):
+        pl.semaphore_signal(barrier, inc=1, device_id=(peer, chan), device_id_type=MESH)
+
+    each_peer(greet)
     for i in range(1, CHANS):
         pl.semaphore_signal(
             barrier, inc=1, device_id=(me, lax.rem(chan + i, CHANS)), device_id_type=MESH
@@ -216,8 +228,7 @@
         return ref.at[pl.ds(pl.multiple_of(i * SLOT, SLOT) + first, count)]
 
     def start(source, target, sent, arrived, first, count):
-        def send(i, c):
-            peer = lax.rem(me + i, BLOCKS)
+        def send(peer):
             pltpu.make_async_remote_copy(
                 src_ref=slot(source, peer, first, count),
                 dst_ref=slot(target, me, first, count),
@@ -226,12 +237,11 @@
                 device_id=(peer, chan),
                 device_id_type=MESH,
             ).start()
-            return c
 
         pltpu.make_async_copy(
             slot(source, me, first, count), slot(target, me, first, count), sent
         ).start()
-        lax.fori_loop(1, BLOCKS, send, 0)
+        each_peer(send)
 
     def finish(source, sent, arrived, count):
         whole = source.at[pl.ds(0, BLOCKS * count)]
@@ -324,6 +334,18 @@
     out_f[...] = total
 
 
+def hand_over(*refs):
+    ins = [pltpu.make_async_copy(refs[i], refs[6 + i], refs[9].at[i]) for i in range(3)]
+    outs = [pltpu.make_async_copy(refs[6 + i], refs[3 + i], refs[10].at[i]) for i in range(3)]
+    for copy in ins:
+        copy.start()
+    for get, put in zip(ins, outs):
+        get.wait()
+        put.start()
+    for copy in outs:
+        copy.wait()
+
+
 def body(signal, filter_taps, skip_gain, cotangent):
     made = tables()
     consts = [signal, cotangent, filter_taps.reshape(A, T), skip_gain]
@@ -332,7 +354,7 @@
     hbm = pl.BlockSpec(memory_space=pltpu.HBM)
     block = jax.ShapeDtypeStruct((ROWS // 2, LOCAL), F32)
     line = jax.ShapeDtypeStruct((A, T), F32)
-    output, grad_signal, grad_filter = pl.pallas_call(
+    results = pl.pallas_call(
         kernel,
         out_shape=(block, block, line),
         in_specs=[hbm] * len(NAMES),
@@ -351,6 +373,16 @@
         ),
         name="hyena",
     )(*consts)
+    output, grad_signal, grad_filter = pl.pallas_call(
+        hand_over,
+        out_shape=(block, block, line),
+        in_specs=[hbm] * 3,
+        out_specs=(hbm,) * 3,
+        scratch_shapes=[pltpu.VMEM(out.shape, F32) for out in (block, block, line)]
+        + [pltpu.SemaphoreType.DMA((3,))] * 2,
+        compiler_params=pltpu.CompilerParams(vmem_limit_bytes=LIMIT),
+        name="hand_over",
+    )(*results)
     return output, grad_signal, grad_filter.reshape(LOCAL)
 
 

time: 51.9 us -> 49.9 us (0.961)
  local copies, waits for them, and re-layouts: 2.78 us -> 0 us
  Pallas kernels: 48.3 us -> 49.1 us
    unnamed x7 -> x0, local copies, waits for them, and re-layouts: 2.78 us -> none
    pallas_call x0 -> x1, Pallas kernels: none -> 1.55 us  [body(): pl.pallas_call(hand_over, out_shape=(block, block, line), in_specs=[hbm]...]
    pallas_call x1, Pallas kernels: 48.3 us -> 47.5 us  [body(): pl.pallas_call(kernel, out_shape=(block, block, line), in_specs=[hbm] * l...]
where the time goes in v2:
time: 49.9 us; the launch traced here: 49.7 us
  Pallas kernels  49.1 us (98%)
  between operations  0.64 us (1%)
    pallas_call x1, Pallas kernels, body(): pl.pallas_call(kernel, out_shape=(block, block, line), in_specs=[hbm] * l...  47.5 us
    pallas_call x1, Pallas kernels, body(): pl.pallas_call(hand_over, out_shape=(block, block, line), in_specs=[hbm]...  1.55 us

profile of v2, /device:TPU:1, one launch (start us, length us, event | category | flops | bytes accessed | tf_op | source)
XLA Modules:
  0.0 49.7 jit_solution(4194743396650244008)
XLA Ops:
  0.6 47.5 %hyena.1 = (f32[16,1024]{1,0:T(8,128)}, f32[16,1024]{1,0:T(8,128)}, f32[8,128]{1,0:T(8,128)}) custom-call(f32[16,1024]{1,0:T(8,128)} %refs_0_.1, f32[16,1024]{1,0:T(8,128)} %refs_1_.1, f32[8,128]{1,0:T(8,128)} %bitcast.2, f32[16]{0:T(128)} %refs_3_.1, f32[2,8,128]{2,1,0:T(8,128)} %constant.18.clone.refs_4_, f32[4,8,128]{2,1,0:T(8,128)} %constant.19.clone.refs_5_, ...), custom_call_target="tpu_custom_call" | custom-call | tf_op jit(solution)/shard_map/hyena/pallas_call | solution.py:357
  48.1 1.6 %hand_over.1 = (f32[16,1024]{1,0:T(8,128)}, f32[16,1024]{1,0:T(8,128)}, f32[8,128]{1,0:T(8,128)}) custom-call(f32[16,1024]{1,0:T(8,128)} %get-tuple-element.9.refs_0_, f32[16,1024]{1,0:T(8,128)} %get-tuple-element.10.refs_1_, f32[8,128]{1,0:T(8,128)} %get-tuple-element.11.refs_2_), custom_call_target="tpu_custom_call" | custom-call | tf_op jit(solution)/shard_map/hand_over/pallas_call | solution.py:376

commit v3 on v2

--- a/solution.py
+++ b/solution.py
@@ -184,9 +184,9 @@
 
 def kernel(*refs):
     n = len(NAMES)
-    sources, (out_s, out_c, out_f) = refs[:n], refs[n : n + 3]
+    sources, results = refs[:n], refs[n : n + 3]
     held = dict(zip(NAMES, refs[n + 3 : 2 * n + 3]))
-    out1, in1, out2, in2, own, others, load, s1, r1, sg, rg, s2, r2, s3, r3 = refs[2 * n + 3 :]
+    out1, in1, out2, in2, own, others, load, s1, r1, sg, rg, s2, r2, s3, r3, out_s, out_c, out_f, leave = refs[2 * n + 3 :]
     me, chan = lax.axis_index("context"), lax.axis_index("chan")
 
     barrier = pltpu.get_barrier_semaphore()
@@ -321,6 +321,12 @@
         at = slice(a * T, (a + 1) * T)
         out_s[:, at] = outs[a][:half] + column * sig[:, at]
         out_c[:, at] = outs[a][half:] + column * cot[:, at]
+    leaves = [
+        pltpu.make_async_copy(made, result, leave.at[i])
+        for i, (made, result) in enumerate(zip((out_s, out_c, out_f), results))
+    ]
+    leaves[0].start()
+    leaves[1].start()
     for copy in copies:
         copy.wait()
     pieces = [own[...]] + [others[i] for i in range(CHANS - 1)]
@@ -332,6 +338,9 @@
             piece = jnp.where(at == i, pieces[i], piece)
         total = total + piece
     out_f[...] = total
+    leaves[2].start()
+    for copy in leaves:
+        copy.wait()
 
 
 def hand_over(*refs):
@@ -350,7 +359,6 @@
     made = tables()
     consts = [signal, cotangent, filter_taps.reshape(A, T), skip_gain]
     consts += [jnp.asarray(made[name]) for name in NAMES[4:]]
-    vmem = pl.BlockSpec(memory_space=pltpu.VMEM)
     hbm = pl.BlockSpec(memory_space=pltpu.HBM)
     block = jax.ShapeDtypeStruct((ROWS // 2, LOCAL), F32)
     line = jax.ShapeDtypeStruct((A, T), F32)
@@ -358,7 +366,7 @@
         kernel,
         out_shape=(block, block, line),
         in_specs=[hbm] * len(NAMES),
-        out_specs=(vmem,) * 3,
+        out_specs=(hbm,) * 3,
         scratch_shapes=[
             (pltpu.SMEM if name == "gain" else pltpu.VMEM)(c.shape, c.dtype)
             for name, c in zip(NAMES, consts)
@@ -367,7 +375,9 @@
         + [pltpu.VMEM((A, T), F32), pltpu.VMEM((CHANS - 1, A, T), F32)]
         + [pltpu.SemaphoreType.DMA((len(NAMES),))]
         + [pltpu.SemaphoreType.DMA] * 6
-        + [pltpu.SemaphoreType.DMA((CHANS - 1,))] * 2,
+        + [pltpu.SemaphoreType.DMA((CHANS - 1,))] * 2
+        + [pltpu.VMEM(out.shape, F32) for out in (block, block, line)]
+        + [pltpu.SemaphoreType.DMA((3,))],
         compiler_params=pltpu.CompilerParams(
             collective_id=0, has_side_effects=True, vmem_limit_bytes=LIMIT
         ),

time: 49.9 us -> 49.9 us (level)
  no operation moved by 1% of the time
where the time goes in v3:
time: 49.9 us; the launch traced here: 49.7 us
  Pallas kernels  49 us (98%)
  between operations  0.64 us (1%)
    pallas_call x1, Pallas kernels, body(): pl.pallas_call(kernel, out_shape=(block, block, line), in_specs=[hbm] * l...  47.5 us
    pallas_call x1, Pallas kernels, body(): pl.pallas_call(hand_over, out_shape=(block, block, line), in_specs=[hbm]...  1.55 us

profile of v3, /device:TPU:1, one launch (start us, length us, event | category | flops | bytes accessed | tf_op | source)
XLA Modules:
  0.0 49.7 jit_solution(3904242045695976850)
XLA Ops:
  0.6 47.5 %hyena.1 = (f32[16,1024]{1,0:T(8,128)}, f32[16,1024]{1,0:T(8,128)}, f32[8,128]{1,0:T(8,128)}) custom-call(f32[16,1024]{1,0:T(8,128)} %refs_0_.1, f32[16,1024]{1,0:T(8,128)} %refs_1_.1, f32[8,128]{1,0:T(8,128)} %bitcast.2, f32[16]{0:T(128)} %refs_3_.1, f32[2,8,128]{2,1,0:T(8,128)} %constant.18.clone.refs_4_, f32[4,8,128]{2,1,0:T(8,128)} %constant.19.clone.refs_5_, ...), custom_call_target="tpu_custom_call" | custom-call | tf_op jit(solution)/shard_map/hyena/pallas_call | solution.py:365
  48.1 1.6 %hand_over.1 = (f32[16,1024]{1,0:T(8,128)}, f32[16,1024]{1,0:T(8,128)}, f32[8,128]{1,0:T(8,128)}) custom-call(f32[16,1024]{1,0:T(8,128)} %get-tuple-element.9.refs_0_, f32[16,1024]{1,0:T(8,128)} %get-tuple-element.10.refs_1_, f32[8,128]{1,0:T(8,128)} %get-tuple-element.11.refs_2_), custom_call_target="tpu_custom_call" | custom-call | tf_op jit(solution)/shard_map/hand_over/pallas_call | solution.py:386
